TPU v7x, 32 devices: a whole 2x2x4 slice. The times are simulated.
32 devices in a mesh: win: 16 (over z, y, x), head: 2 (over core).
Axes of the slice: x: 2, y: 2, z: 4, core: 2. Of those that a mesh axis runs over, the one named last changes fastest.
Arguments:
- coords: float32 [3, 512, 128], P(None, 'win', 'head'), may hold values from -8 to 16
- noise: float32 [3, 512, 128], P(None, 'win', 'head'), may hold values from -6 to 6
- sigma: float32 [1], replicated, may hold values from 0.25 to 1
- atom_single: bfloat16 [512, 128, 128], P('win', 'head'), may hold values from -6 to 6
- token_single: bfloat16 [8192, 384], P('win'), may hold values from -6 to 6
- atom_token: int32 [512, 128], P('win', 'head'), may hold values from 0 to 15, never falling along the last dimension, each value on 1 to 64 neighbouring positions
- window_count: int32 [16], replicated, may hold values from 1 to 31, as said below
- pair_bias: bfloat16 [4, 512, 128, 128], P('head', 'win'), may hold values from -6 to 260
- token_weight: bfloat16 [384, 128], replicated, may hold values from -0.3125 to 0.3125
- cond_gain: float32 [128], replicated, may hold values from 0.25 to 1.75
- position_weight: float32 [3, 128], replicated, may hold values from -3.5 to 3.5
- ada_weight: bfloat16 [3, 6, 128, 128], replicated, may hold values from -0.5 to 0.5
- ada_bias: float32 [3, 6, 128], replicated, may hold values from -4 to 4
- attn_weight: bfloat16 [3, 4, 128, 128], P(None, None, None, 'head'), may hold values from -0.5 to 0.5
- out_weight: bfloat16 [3, 128, 128], P(None, 'head'), may hold values from -0.5 to 0.5
- gateup_weight: bfloat16 [3, 2, 128, 256], replicated, may hold values from -0.5 to 0.5
- down_weight: bfloat16 [3, 256, 128], replicated, may hold values from -0.375 to 0.375
- final_weight: bfloat16 [3, 128], replicated, may hold values from -0.5 to 0.5
Outputs:
- denoised: float32 [3, 512, 128], P(None, 'win', 'head')
Inputs may be any that keep to these rules, and one draw needn't show every extreme that they name: window_count[d] + window_count[d + 8] <= 32 for every d < 8, with equality for some d.
All inputs are finite; a program needn't handle non-finite values.
Results may differ from a plain program's by a relative error of at most 0.005.
Values may be sent and summed in bfloat16 or wider, within the bound.
No kernel may reach another device: no remote copies, remote signals or barrier semaphores. Data moves between devices by JAX's collectives and lax.ppermute only.
A program may use at most 128 MiB of HBM per device.

v0:
```python
import jax
import jax.numpy as jnp
from jax import lax
from jax.sharding import PartitionSpec as P

HEAD_DIM = 32
QW = 128
TOKW = 16
BLOCKS = 3


EPSILON = 1e-05


def layer_norm(values):
    average = jnp.mean(values, axis=-1, keepdims=True)
    centred = values - average
    variance = jnp.mean(centred * centred, axis=-1, keepdims=True)
    return centred * lax.rsqrt(variance + EPSILON)


def lookup_tokens(tokens_here, local_token):
    token_grid = tokens_here.reshape(local_token.shape[0], TOKW, -1)
    one_hot = (local_token[:, :, None] == jnp.arange(TOKW, dtype=jnp.int32)).astype(jnp.bfloat16)
    return jnp.einsum(
        "wqt,wtc->wqc", one_hot, token_grid, preferred_element_type=jnp.float32
    ).astype(jnp.bfloat16)


def project_rows(weight_set, portion):
    return jnp.einsum(
        "wqc,jcd->jwqd", portion, weight_set, preferred_element_type=jnp.float32
    ).astype(jnp.bfloat16)


def window_net(single, looked, scaled, pair_terms, weights_all, project_fn, output_fn):
    cond_gain, position_weight, ada_weight, ada_bias, gateup_weight, down_weight, final_weight = (
        weights_all
    )
    condition = single.astype(jnp.float32) + looked.astype(jnp.float32)
    cond_norm = (layer_norm(condition) * cond_gain).astype(jnp.bfloat16)
    stream = condition + jnp.einsum(
        "kwq,kc->wqc", scaled, position_weight, precision=lax.Precision.HIGHEST
    )
    window_total = single.shape[0]
    for block_index in range(BLOCKS):
        ada_terms = (
            jnp.einsum(
                "wqc,jcd->jwqd",
                cond_norm,
                ada_weight[block_index],
                preferred_element_type=jnp.float32,
            )
            + ada_bias[block_index][:, None, None, :]
        )
        normed = (layer_norm(stream) * jax.nn.sigmoid(ada_terms[0]) + ada_terms[1]).astype(
            jnp.bfloat16
        )
        projected = project_fn(block_index, normed)
        row_count = projected.shape[2]
        query_rows = projected[0].reshape(window_total, row_count, -1, HEAD_DIM)
        key_rows = projected[1].reshape(window_total, row_count, -1, HEAD_DIM)
        value_rows = projected[2].reshape(window_total, row_count, -1, HEAD_DIM)
        gate_logits = (
            projected[3].reshape(window_total, row_count, -1, HEAD_DIM).astype(jnp.float32)
        )
        scores = jnp.einsum(
            "wqhd,wkhd->hwqk", query_rows, key_rows, preferred_element_type=jnp.float32
        )
        scores = scores * HEAD_DIM ** (-0.5) + pair_terms.astype(jnp.float32)
        row_max = jnp.max(scores, axis=-1, keepdims=True)
        exponent = jnp.exp(scores - row_max)
        weights = (exponent / jnp.sum(exponent, axis=-1, keepdims=True)).astype(jnp.bfloat16)
        attended = jnp.einsum(
            "hwqk,wkhd->wqhd", weights, value_rows, preferred_element_type=jnp.float32
        )
        attended = (
            (attended * jax.nn.sigmoid(gate_logits))
            .astype(jnp.bfloat16)
            .reshape(window_total, row_count, -1)
        )
        update = output_fn(block_index, attended)
        stream = stream + jax.nn.sigmoid(ada_terms[2]) * update
        normed_two = (layer_norm(stream) * jax.nn.sigmoid(ada_terms[3]) + ada_terms[4]).astype(
            jnp.bfloat16
        )
        gate_part = jnp.einsum(
            "wqc,ch->wqh",
            normed_two,
            gateup_weight[block_index, 0],
            preferred_element_type=jnp.float32,
        )
        up_part = jnp.einsum(
            "wqc,ch->wqh",
            normed_two,
            gateup_weight[block_index, 1],
            preferred_element_type=jnp.float32,
        )
        hidden = (jax.nn.silu(gate_part) * up_part).astype(jnp.bfloat16)
        down_part = jnp.einsum(
            "wqh,hc->wqc", hidden, down_weight[block_index], preferred_element_type=jnp.float32
        )
        stream = stream + jax.nn.sigmoid(ada_terms[5]) * down_part
    final_norm = layer_norm(stream).astype(jnp.bfloat16)
    return jnp.einsum("wqc,kc->kwq", final_norm, final_weight, preferred_element_type=jnp.float32)


def run_net(single, looked, scaled, pair_terms, weights_all, attn_weight, out_weight):
    attn_full, out_full = (
        lax.all_gather(attn_weight, "head", axis=3, tiled=True),
        lax.all_gather(out_weight, "head", axis=1, tiled=True),
    )
    single_own, looked_own = (
        lax.all_to_all(single, "head", split_axis=0, concat_axis=1, tiled=True),
        lax.all_to_all(looked, "head", split_axis=0, concat_axis=1, tiled=True),
    )
    terms_own = lax.all_to_all(pair_terms, "head", split_axis=1, concat_axis=0, tiled=True)
    scaled_own = lax.all_to_all(scaled, "head", split_axis=1, concat_axis=2, tiled=True)

    def project_local(block_index, normed):
        return project_rows(attn_full[block_index], normed)

    def output_local(block_index, attended):
        return jnp.einsum(
            "wqd,dc->wqc", attended, out_full[block_index], preferred_element_type=jnp.float32
        )

    update_own = window_net(
        single_own, looked_own, scaled_own, terms_own, weights_all, project_local, output_local
    )
    return lax.all_to_all(update_own, "head", split_axis=2, concat_axis=1, tiled=True)


def local(
    coords,
    noise,
    sigma,
    atom_single,
    token_single,
    atom_token,
    window_count,
    pair_bias,
    token_weight,
    cond_gain,
    position_weight,
    ada_weight,
    ada_bias,
    attn_weight,
    out_weight,
    gateup_weight,
    down_weight,
    final_weight,
):
    sigma_value = sigma[0]
    noisy_pos = coords + sigma_value * noise
    slot_total = atom_single.shape[0]
    device_id = lax.axis_index("win")
    own_count = window_count[device_id]
    slot_ids = jnp.arange(slot_total, dtype=jnp.int32)
    live_mask = (slot_ids < own_count).astype(jnp.float32)
    partial_pos = jnp.sum(noisy_pos * live_mask[None, :, None], axis=(1, 2))
    totals = lax.psum(partial_pos, ("win", "head"))
    centre = totals / (QW * jnp.sum(window_count).astype(jnp.float32))
    shifted = noisy_pos - centre[:, None, None]
    inverse = 1.0 / (1.0 + sigma_value * sigma_value)
    scaled = shifted * jnp.sqrt(inverse)
    token_proj = jnp.dot(token_single, token_weight, preferred_element_type=jnp.float32).astype(
        jnp.bfloat16
    )
    looked = lookup_tokens(token_proj, atom_token)
    weights_all = (
        cond_gain,
        position_weight,
        ada_weight,
        ada_bias,
        gateup_weight,
        down_weight,
        final_weight,
    )
    update_pos = run_net(
        atom_single, looked, scaled, pair_bias, weights_all, attn_weight, out_weight
    )
    denoised = shifted * inverse + sigma_value * jnp.sqrt(inverse) * update_pos
    return denoised * live_mask[None, :, None]


def solution(mesh):
    placed = (
        P(None, "win", "head"),
        P(None, "win", "head"),
        P(),
        P("win", "head", None),
        P("win", None),
        P("win", "head"),
        P(),
        P("head", "win", None, None),
        P(),
        P(),
        P(),
        P(),
        P(),
        P(None, None, None, "head"),
        P(None, "head", None),
        P(),
        P(),
        P(),
    )
    return jax.shard_map(
        local, mesh=mesh, in_specs=placed, out_specs=P(None, "win", "head"), check_vma=False
    )
```

profile of v0, /device:TPU:0, one launch (start us, length us, event | category | flops | bytes accessed | tf_op | source)
XLA Modules:
  0.0 158.0 jit_solution(3100987387684323623)
XLA Ops:
  4.1 3.5 %all-to-all-start.1 = ((bf16[32,64,128]{2,1,0:T(8,128)(2,1)}), bf16[32,64,128]{2,1,0:T(8,128)(2,1)S(1)}, u32[]{:S(2)}, u32[]{:S(2)}) async-start(bf16[32,64,128]{2,1,0:T(8,128)(2,1)} %convolution_convert_fusion), calls=%async_computation.1 | async-start | bytes 1048576 | tf_op jit(solution)/shard_map/all_to_all | solution.py:115
  12.7 42.0 %psum.7 = f32[3]{0:T(128)S(1)} all-reduce(f32[3]{0:T(128)S(1)} %get-tuple-element.5), channel_id=1, replica_groups=mesh['win'=16,'head'=2] {'win','head'}, use_global_device_ids=true, to_apply=%region_1.0 | all-reduce | flops 3 | bytes 24 | tf_op jit(solution)/shard_map/psum | solution.py:162
  56.6 5.2 %all_to_all.54 = bf16[32,64,128]{2,1,0:T(8,128)(2,1)S(1)} all-to-all(bf16[32,64,128]{2,1,0:T(8,128)(2,1)} %param.21), channel_id=1, replica_groups=mesh['win'=16,'head'=2] {'head'}, dimensions={0} | all-to-all | bytes 1048576 | tf_op jit(solution)/shard_map/all_to_all | solution.py:114
  61.9 3.2 %all-to-all-start.2 = ((f32[2,1,3072]{2,1,0:T(1,128)}), f32[2,1,3072]{2,1,0:T(1,128)S(1)}, u32[]{:S(2)}, u32[]{:S(2)}) async-start(f32[2,1,3072]{2,1,0:T(1,128)} %reshape.288), calls=%async_computation.2 | async-start | bytes 49152 | tf_op jit(solution)/shard_map/all_to_all | solution.py:118
  67.1 3.3 %copy.241 = bf16[2,32,128,128]{3,2,0,1:T(8,128)(2,1)} copy(bf16[2,32,128,128]{3,2,1,0:T(8,128)(2,1)} %param.25) | data formatting | bytes 4194304 | tf_op args[7]
  70.4 5.0 %all-to-all-start.3 = ((bf16[2,32,128,128]{3,2,0,1:T(8,128)(2,1)}), bf16[2,32,128,128]{3,2,0,1:T(8,128)(2,1)}, u32[]{:S(2)}, u32[]{:S(2)}) async-start(bf16[2,32,128,128]{3,2,0,1:T(8,128)(2,1)} %copy.241), calls=%async_computation.3 | async-start | bytes 4194304 | tf_op jit(solution)/shard_map/all_to_all | solution.py:117
  77.7 2.3 %fusion.184 = (f32[16,128]{1,0:T(8,128)S(1)}, f32[16,128,128]{1,2,0:T(8,128)S(1)}) fusion(f32[16,128,128]{1,2,0:T(8,128)} %copy.234, f32[3,128]{1,0:T(4,128)S(1)} %copy-done.13, f32[3,16,128]{2,1,0:T(8,128)S(1)} %all_to_all.21), kind=kOutput, calls=%fused_computation.250 | convolution fusion | flops 9959424 | bytes 2131456 | tf_op jit(solution)/shard_map/kwq,kc->wqc/dot_general | solution.py:42
  80.1 2.2 %all_gather.6 = bf16[3,4,128,128]{2,3,1,0:T(8,128)(2,1)S(1)} all-gather(bf16[3,4,128,64]{2,3,1,0:T(8,128)(2,1)S(1)} %copy-done.9), channel_id=1, replica_groups=mesh['win'=16,'head'=2] {'head'}, dimensions={3}, use_global_device_ids=true | all-gather | bytes 589824 | tf_op jit(solution)/shard_map/all_gather | solution.py:110
  88.1 4.2 %copy.242 = f32[2,2,16,128,128]{3,4,2,0,1:T(8,128)} copy(bf16[2,2,16,128,128]{4,3,0,2,1:T(8,128)(2,1)} %bitcast.113) | data formatting | bytes 6291456 | tf_op jit(solution)/shard_map/convert_element_type | solution.py:70
  92.3 3.0 %bitcast_add_fusion.2 = f32[4,16,128,128]{2,3,1,0:T(8,128)S(1)} fusion(f32[2,2,16,128,128]{3,4,2,0,1:T(8,128)} %copy.242, bf16[16,128,4,32]{1,3,2,0:T(8,128)(2,1)S(1)} %bitcast.382, bf16[16,128,4,32]{1,3,2,0:T(8,128)(2,1)S(1)} %bitcast.381), kind=kOutput, calls=%fused_computation.8 | convolution fusion | flops 69206016 | bytes 9437184 | tf_op jit(solution)/shard_map/wqhd,wkhd->hwqk/dot_general | solution.py:67
  95.3 3.9 %fusion.185 = (f32[4,16,128]{2,1,0:T(8,128)S(1)}, f32[4,16,128,128]{2,3,1,0:T(8,128)S(1)}) fusion(f32[4,16,128,128]{2,3,1,0:T(8,128)S(1)} %bitcast_add_fusion.2), kind=kOutput, calls=%fused_computation.251 | output fusion | flops 2097279 | bytes 8421376 | tf_op jit(solution)/shard_map/sub | solution.py:72
  99.2 2.1 %all_gather.7 = bf16[3,128,128]{2,1,0:T(8,128)(2,1)S(1)} all-gather(bf16[3,64,128]{2,1,0:T(8,128)(2,1)S(1)} %copy-done.11), channel_id=1, replica_groups=mesh['win'=16,'head'=2] {'head'}, dimensions={1}, use_global_device_ids=true | all-gather | bytes 147456 | tf_op jit(solution)/shard_map/all_gather | solution.py:111
  104.5 4.6 %add_bitcast_fusion.1 = f32[6,16,128,128]{2,3,1,0:T(8,128)} fusion(f32[6,128]{1,0:T(8,128)S(1)} %get-tuple-element.18, bf16[16,128,128,1]{2,1,0,3:T(8,128)(2,1)S(1)} %bitcast.378, bf16[3,6,128,128]{3,2,1,0:T(8,128)(2,1)} %param.29), kind=kOutput, calls=%fused_computation.4 | convolution fusion | flops 404226048 | bytes 7015424 | tf_op jit(solution)/shard_map/wqc,jcd->jwqd/dot_general | solution.py:48
  109.1 2.7 %fusion.155 = f32[16,128,256]{2,1,0:T(8,128)} fusion(bf16[16,128,128]{1,2,0:T(8,128)(2,1)S(1)} %fusion.93, bf16[3,2,128,256]{3,2,1,0:T(8,128)(2,1)} %param.33), kind=kOutput, calls=%fused_computation.195 | convolution fusion | flops 134217728 | bytes 2686976 | tf_op jit(solution)/shard_map/wqc,ch->wqh/dot_general | solution.py:93
  111.7 3.0 %fusion.187 = (f32[16,128]{1,0:T(8,128)S(1)}, f32[16,128,128]{1,2,0:T(8,128)S(1)}) fusion(f32[16,128,128]{1,2,0:T(8,128)S(1)} %get-tuple-element.24, bf16[3,256,128]{2,1,0:T(8,128)(2,1)} %param.34, f32[16,128,256]{2,1,0:T(8,128)} %fusion.155, bf16[16,128,128]{1,2,0:T(8,128)(2,1)S(1)} %fusion.93, bf16[3,2,128,256]{3,2,1,0:T(8,128)(2,1)} %param.33, ...), kind=kOutput, calls=%fused_computation.253 | convolution fusion | flops 273152000 | bytes 5906432 | tf_op jit(solution)/shard_map/wqh,hc->wqc/dot_general | solution.py:100
  114.9 2.5 %convert_bitcast_fusion.1 = bf16[4,16,128,128]{2,3,1,0:T(8,128)(2,1)S(1)} fusion(f32[6,16,128,128]{2,3,1,0:T(8,128)} %add_bitcast_fusion.1, f32[16,128,128]{1,2,0:T(8,128)S(1)} %get-tuple-element.26, f32[16,128]{1,0:T(8,128)S(1)} %add_rsqrt_fusion.5, f32[16,128]{1,0:T(8,128)S(1)} %broadcast_multiply_fusion.6, bf16[3,4,128,128]{2,3,1,0:T(8,128)(2,1)S(1)} %all_gather.6), kind=kOutput, calls=%fused_computation.24 | convolution fusion | flops 271581184 | bytes 5390336 | tf_op jit(solution)/shard_map/wqc,jcd->jwqd/dot_general | solution.py:31
  118.6 4.1 %fusion.190 = (f32[4,16,128]{2,1,0:T(8,128)S(1)}, f32[4,16,128,128]{2,3,1,0:T(8,128)S(1)}) fusion(f32[4,16,128,128]{2,3,1,0:T(8,128)S(1)} %bitcast_add_fusion.1), kind=kOutput, calls=%fused_computation.254 | output fusion | flops 2097279 | bytes 8421376 | tf_op jit(solution)/shard_map/sub | solution.py:72
  126.7 2.7 %fusion.151 = f32[16,128,256]{2,1,0:T(8,128)} fusion(bf16[16,128,128]{1,2,0:T(8,128)(2,1)S(1)} %fusion.71, bf16[3,2,128,256]{3,2,1,0:T(8,128)(2,1)} %param.33), kind=kOutput, calls=%fused_computation.192 | convolution fusion | flops 134217728 | bytes 2686976 | tf_op jit(solution)/shard_map/wqc,ch->wqh/dot_general | solution.py:93
  129.3 3.0 %fusion.192 = (f32[16,128]{1,0:T(8,128)S(1)}, f32[16,128,128]{1,2,0:T(8,128)S(1)}) fusion(f32[16,128,128]{1,2,0:T(8,128)S(1)} %get-tuple-element.30, bf16[3,256,128]{2,1,0:T(8,128)(2,1)} %param.34, f32[16,128,256]{2,1,0:T(8,128)} %fusion.151, bf16[16,128,128]{1,2,0:T(8,128)(2,1)S(1)} %fusion.71, bf16[3,2,128,256]{3,2,1,0:T(8,128)(2,1)} %param.33, ...), kind=kOutput, calls=%fused_computation.256 | convolution fusion | flops 273152000 | bytes 5906432 | tf_op jit(solution)/shard_map/wqh,hc->wqc/dot_general | solution.py:100
  135.7 3.1 %copy-done.3 = f32[2,2,16,128,128]{3,4,2,0,1:T(8,128)S(1)} copy-done((f32[2,2,16,128,128]{3,4,2,0,1:T(8,128)S(1)}, f32[2,2,16,128,128]{3,4,2,0,1:T(8,128)}, u32[]{:S(2)}) %copy-start.3) | copy-done | bytes 4194328
  139.5 3.9 %fusion.195 = (f32[4,16,128]{2,1,0:T(8,128)S(1)}, f32[4,16,128,128]{2,3,1,0:T(8,128)S(1)}) fusion(f32[4,16,128,128]{2,3,1,0:T(8,128)S(1)} %bitcast_add_fusion), kind=kOutput, calls=%fused_computation.257 | output fusion | flops 2097279 | bytes 8421376 | tf_op jit(solution)/shard_map/sub | solution.py:72
  145.9 2.6 %fusion.147 = f32[16,128,256]{2,1,0:T(8,128)} fusion(bf16[16,128,128]{1,2,0:T(8,128)(2,1)S(1)} %fusion.49, bf16[3,2,128,256]{3,2,1,0:T(8,128)(2,1)} %param.33), kind=kOutput, calls=%fused_computation.189 | convolution fusion | flops 134217728 | bytes 2686976 | tf_op jit(solution)/shard_map/wqc,ch->wqh/dot_general | solution.py:93
  148.5 3.0 %fusion.197 = (f32[16,128]{1,0:T(8,128)S(1)}, f32[16,128,128]{1,2,0:T(8,128)S(1)}) fusion(f32[16,128,128]{1,2,0:T(8,128)S(1)} %get-tuple-element.36, bf16[3,256,128]{2,1,0:T(8,128)(2,1)} %param.34, f32[16,128,256]{2,1,0:T(8,128)} %fusion.147, bf16[16,128,128]{1,2,0:T(8,128)(2,1)S(1)} %fusion.49, bf16[3,2,128,256]{3,2,1,0:T(8,128)(2,1)} %param.33, ...), kind=kOutput, calls=%fused_computation.259 | convolution fusion | flops 273152000 | bytes 5906432 | tf_op jit(solution)/shard_map/wqh,hc->wqc/dot_general | solution.py:100
  152.3 3.7 %all_to_all.55 = f32[2,1,3072]{2,1,0:T(1,128)S(1)} all-to-all(f32[2,1,3072]{2,1,0:T(1,128)S(1)} %reshape.290), channel_id=1, replica_groups=mesh['win'=16,'head'=2] {'head'}, dimensions={0} | all-to-all | bytes 49152 | tf_op jit(solution)/shard_map/all_to_all | solution.py:131
  (124 shorter events, 37.2 us)
Async XLA Ops:
  0.0 1.0 copy-start
  4.1 52.5 %all-to-all-start.1 = ((bf16[32,64,128]{2,1,0:T(8,128)(2,1)}), bf16[32,64,128]{2,1,0:T(8,128)(2,1)S(1)}, u32[]{:S(2)}, u32[]{:S(2)}) async-start(bf16[32,64,128]{2,1,0:T(8,128)(2,1)} %convolution_convert_fusion), calls=%async_computation.1 | async-start | bytes 1048576 | tf_op jit(solution)/shard_map/all_to_all | solution.py:115
  12.6 54.5 %copy-start.7 = (f32[3,32,64]{2,1,0:T(8,128)}, f32[3,32,64]{2,1,0:T(8,128)S(1)}, u32[]{:S(2)}) copy-start(f32[3,32,64]{2,1,0:T(8,128)S(1)} %get-tuple-element.6) | copy-start | bytes 73732
  61.9 8.5 %all-to-all-start.2 = ((f32[2,1,3072]{2,1,0:T(1,128)}), f32[2,1,3072]{2,1,0:T(1,128)S(1)}, u32[]{:S(2)}, u32[]{:S(2)}) async-start(f32[2,1,3072]{2,1,0:T(1,128)} %reshape.288), calls=%async_computation.2 | async-start | bytes 49152 | tf_op jit(solution)/shard_map/all_to_all | solution.py:118
  67.1 9.8 %copy-start.12 = (f32[3,6,128]{2,1,0:T(8,128)S(1)}, f32[3,6,128]{2,1,0:T(8,128)}, u32[]{:S(2)}) copy-start(f32[3,6,128]{2,1,0:T(8,128)} %param.30) | copy-start | bytes 27652
  67.1 10.5 %copy-start.13 = (f32[3,128]{1,0:T(4,128)S(1)}, f32[3,128]{1,0:T(4,128)}, u32[]{:S(2)}) copy-start(f32[3,128]{1,0:T(4,128)} %param.28) | copy-start | bytes 4612
  70.4 9.7 %copy-start.9 = (bf16[3,4,128,64]{2,3,1,0:T(8,128)(2,1)S(1)}, bf16[3,4,128,64]{2,3,1,0:T(8,128)(2,1)}, u32[]{:S(2)}) copy-start(bf16[3,4,128,64]{2,3,1,0:T(8,128)(2,1)} %param.31) | copy-start | bytes 589828
  70.4 11.9 %copy-start.17 = (f32[128]{0:T(128)S(1)}, f32[128]{0:T(128)}, u32[]{:S(2)}) copy-start(f32[128]{0:T(128)} %param.27) | copy-start | bytes 1540
  70.4 17.7 %all-to-all-start.3 = ((bf16[2,32,128,128]{3,2,0,1:T(8,128)(2,1)}), bf16[2,32,128,128]{3,2,0,1:T(8,128)(2,1)}, u32[]{:S(2)}, u32[]{:S(2)}) async-start(bf16[2,32,128,128]{3,2,0,1:T(8,128)(2,1)} %copy.241), calls=%async_computation.3 | async-start | bytes 4194304 | tf_op jit(solution)/shard_map/all_to_all | solution.py:117
  85.0 3.0 %copy-start.4 = (f32[6,16,128,128]{2,3,1,0:T(8,128)}, f32[6,16,128,128]{2,3,1,0:T(8,128)S(1)}, u32[]{:S(2)}) copy-start(f32[6,16,128,128]{2,3,1,0:T(8,128)S(1)} %add_bitcast_fusion.2) | copy-start | bytes 18874372
  95.2 4.0 %copy-start.11 = (bf16[3,64,128]{2,1,0:T(8,128)(2,1)S(1)}, bf16[3,64,128]{2,1,0:T(8,128)(2,1)}, u32[]{:S(2)}) copy-start(bf16[3,64,128]{2,1,0:T(8,128)(2,1)} %param.32) | copy-start | bytes 147460
  95.2 6.0 %copy-start.6 = (f32[1,16,128,128]{2,3,1,0:T(8,128)S(1)}, f32[1,16,128,128]{2,3,1,0:T(8,128)}, u32[]{:S(2)}) copy-start(f32[1,16,128,128]{2,3,1,0:T(8,128)} %add_divide_fusion.2) | copy-start | bytes 3145732
  95.3 6.7 %slice-start.2 = ((s8[6291456]{0:T(1024)(128)(4,1)}), s8[2097152]{0:T(1024)(128)(4,1)S(1)}, s32[]{:S(2)}) async-start(s8[6291456]{0:T(1024)(128)(4,1)} %bitcast.375), calls=%async_computation.7 | async-start | bytes 4194304
  101.3 0.7 copy-start.10
  101.3 2.2 %slice-start.3 = ((s8[6291456]{0:T(1024)(128)(4,1)}), s8[4194304]{0:T(1024)(128)(4,1)S(1)}, s32[]{:S(2)}) async-start(s8[6291456]{0:T(1024)(128)(4,1)} %bitcast.375), calls=%async_computation.8 | async-start | bytes 8388608
  114.9 2.9 %copy-start.2 = (f32[2,2,16,128,128]{3,4,2,0,1:T(8,128)S(1)}, f32[2,2,16,128,128]{3,4,2,0,1:T(8,128)}, u32[]{:S(2)}) copy-start(f32[2,2,16,128,128]{3,4,2,0,1:T(8,128)} %copy.242) | copy-start | bytes 12582916
  118.6 4.8 %slice-start = ((s8[6291456]{0:T(1024)(128)(4,1)}), s8[2097152]{0:T(1024)(128)(4,1)S(1)}, s32[]{:S(2)}) async-start(s8[6291456]{0:T(1024)(128)(4,1)} %bitcast.373), calls=%async_computation.5 | async-start | bytes 4194304
  122.7 2.2 %slice-start.1 = ((s8[6291456]{0:T(1024)(128)(4,1)}), s8[4194304]{0:T(1024)(128)(4,1)S(1)}, s32[]{:S(2)}) async-start(s8[6291456]{0:T(1024)(128)(4,1)} %bitcast.373), calls=%async_computation.6 | async-start | bytes 8388608
  134.3 11.2 %copy-start.5 = (f32[6,16,128,128]{2,3,1,0:T(8,128)}, f32[6,16,128,128]{2,3,1,0:T(8,128)S(1)}, u32[]{:S(2)}) copy-start(f32[6,16,128,128]{2,3,1,0:T(8,128)S(1)} %add_bitcast_fusion) | copy-start | bytes 18874372
  134.4 4.3 %copy-start.3 = (f32[2,2,16,128,128]{3,4,2,0,1:T(8,128)S(1)}, f32[2,2,16,128,128]{3,4,2,0,1:T(8,128)}, u32[]{:S(2)}) copy-start(f32[2,2,16,128,128]{3,4,2,0,1:T(8,128)} %copy.242) | copy-start | bytes 12582916
  148.5 3.2 %copy-start.16 = (bf16[3,128]{1,0:T(4,128)(2,1)S(1)}, bf16[3,128]{1,0:T(4,128)(2,1)}, u32[]{:S(2)}) copy-start(bf16[3,128]{1,0:T(4,128)(2,1)} %param.35) | copy-start | bytes 2308
  148.5 8.7 %copy-start.8 = (f32[3,32,64]{2,1,0:T(8,128)S(1)}, f32[3,32,64]{2,1,0:T(8,128)}, u32[]{:S(2)}) copy-start(f32[3,32,64]{2,1,0:T(8,128)} %copy-done.7) | copy-start | bytes 73732
  148.5 8.7 %copy-start.15 = (f32[3]{0:T(128)S(1)}, f32[3]{0:T(128)}, u32[]{:S(2)}) copy-start(f32[3]{0:T(128)} %copy-done.14) | copy-start | bytes 40
  148.5 9.4 %copy-start.1 = (bf16[512,384]{1,0:T(8,128)(2,1)S(1)}, bf16[512,384]{1,0:T(8,128)(2,1)}, u32[]{:S(2)}) copy-start(bf16[512,384]{1,0:T(8,128)(2,1)} %param.22) | copy-start | bytes 1179652
  (1 other events, 0.5 us)
where the time goes:
time: 159 us; the launch traced here: 158 us
  blocking collectives  55.2 us (35%)
  matrix products  44.6 us (28%)
  other arithmetic  23.5 us (15%)
  local copies, waits for them, and re-layouts  20.9 us (13%)
  starting transfers between devices  11.7 us (7%)
  between operations  2.11 us (1%)
    psum x1, blocking collectives, local(): totals = lax.psum(partial_pos, ('win', 'head'))  42 us
    unnamed x49, local copies, waits for them, and re-layouts  12.6 us
    sub x3, other arithmetic, window_net(): exponent = jnp.exp(scores - row_max)  12 us
    dot_general x3, matrix products, window_net(): jnp.einsum('wqh,hc->wqc', hidden, down_weight[block_index], preferred_ele...  9.03 us
    dot_general x3, matrix products, window_net(): jnp.einsum('wqc,jcd->jwqd', cond_norm, ada_weight[block_index], preferred...  8.5 us
    dot_general x3, matrix products, window_net(): jnp.einsum('wqc,ch->wqh', normed_two, gateup_weight[block_index, 1], pref...  7.96 us
    all_to_all x1, blocking collectives, run_net(): lax.all_to_all(single, 'head', split_axis=0, concat_axis=1, tiled=True)  5.22 us
    all_to_all x1, starting transfers between devices, run_net(): lax.all_to_all(pair_terms, 'head', split_axis=1, concat_axis=0, tiled=True)  4.97 us
  transfers between devices with their start and end apart: 3, of which 0 were waited for; matrix products, arithmetic and copies ran while one was open for 13% of the time, Pallas kernels for 0%

commit v1 on v0

v1 whole, which is shorter than its diff:
```python
import functools

import jax
import jax.numpy as jnp
from jax import lax
from jax.experimental import pallas as pl
from jax.experimental.pallas import tpu as pltpu
from jax.sharding import PartitionSpec as P

HEAD_DIM = 32
QW = 128
TOKW = 16
BLOCKS = 3
HEADS = 4
GROUP = 4

EPSILON = 1e-05
F32 = jnp.float32
BF16 = jnp.bfloat16


def dot(left, right):
    return jnp.dot(left, right, preferred_element_type=F32)


def dot_nt(left, right):
    return lax.dot_general(left, right, (((1,), (1,)), ((), ())), preferred_element_type=F32)


def eye(size):
    rows = lax.broadcasted_iota(jnp.int32, (size, size), 0)
    columns = lax.broadcasted_iota(jnp.int32, (size, size), 1)
    return jnp.where(rows == columns, 1.0, 0.0).astype(BF16)


def split(value):
    high = value.astype(BF16).astype(F32)
    rest = value - high
    middle = rest.astype(BF16).astype(F32)
    return high, middle, rest - middle


def centred(values):
    average = jnp.mean(values, axis=0, keepdims=True)
    rest = values - average
    variance = jnp.mean(rest * rest, axis=0, keepdims=True)
    return rest, lax.rsqrt(variance + EPSILON)


def prepare(
    weights, ada_t, attn_t, out_t, gateup_t, down_t, token_t, position_l, gain_b
):
    (ada, ada_bias, attn_own, attn_other, out_own, out_other, gateup, down, token, position, gain) = weights
    one = eye(QW)
    small = eye(QW // 2)

    def block(b, carry):
        for j in range(6):
            factor = 1.0 if j in (1, 4) else 0.5
            bias = ada_bias[b, pl.ds(j, 1), :]
            high, middle, low = split(bias)
            pad = jnp.zeros((7, QW), F32)
            tail = jnp.concatenate(
                [high, pad, middle, pad, low, pad, jnp.zeros((QW - 24, QW), F32)], axis=0
            ).astype(BF16)
            whole = jnp.concatenate([ada[b, j], tail], axis=0)
            ada_t[b, pl.ds(j * QW, QW), :] = (dot_nt(one, whole) * factor).astype(BF16)
        for j in range(4):
            factor = 0.5 if j == 3 else 1.0
            for half, part in enumerate((attn_own, attn_other)):
                attn_t[b, pl.ds(j * QW + half * 64, 64), :] = (dot_nt(small, part[b, j]) * factor).astype(BF16)
        out = jnp.concatenate([out_own[b], out_other[b]], axis=0)
        out_t[b] = (dot_nt(one, out) * 0.25).astype(BF16)
        for j in range(2):
            factor = 0.5 if j == 0 else 1.0
            for half in range(2):
                part = gateup[b, j, :, pl.ds(half * QW, QW)]
                gateup_t[b, pl.ds((2 * j + half) * QW, QW), :] = (dot_nt(one, part) * factor).astype(BF16)
        down_t[b] = (dot_nt(one, down[b]) * 0.5).astype(BF16)
        return carry

    lax.fori_loop(0, BLOCKS, block, 0)
    token_t[...] = dot_nt(one, token[...]).astype(BF16)
    high, middle, low = split(position[...])
    parts = jnp.concatenate([high, middle, low, high, middle, high], axis=0).astype(BF16)
    position_l[...] = dot_nt(one, parts).astype(BF16)
    gain_b[...] = jnp.broadcast_to(gain[...], (QW, QW))


def network(
    core_ref,
    single_own,
    single_other,
    tokens,
    rows_ref,
    bias_own,
    bias_other,
    ada,
    ada_bias,
    attn_own,
    attn_other,
    out_own,
    out_other,
    gateup,
    down,
    token,
    position,
    gain,
    final,
    result,
    ada_t,
    attn_t,
    out_t,
    gateup_t,
    down_t,
    token_t,
    position_l,
    gain_b,
    single_s,
    bias_t,
    cond_s,
    stream_s,
):
    @pl.when(pl.program_id(0) == 0)
    def _():
        prepare(
            (ada, ada_bias, attn_own, attn_other, out_own, out_other, gateup, down, token, position, gain),
            ada_t, attn_t, out_t, gateup_t, down_t, token_t, position_l, gain_b,
        )

    core = core_ref[0]
    one = eye(QW)
    wide = GROUP * QW
    own_row = pl.multiple_of(core * 64, 64)
    other_row = pl.multiple_of(64 - core * 64, 64)
    for w in range(GROUP):
        single_s[w, pl.ds(own_row, 64), :] = single_own[w]
        single_s[w, pl.ds(other_row, 64), :] = single_other[w]
        for h in range(HEADS):
            part = bias_own[h, w] if h < 2 else bias_other[h - 2, w]
            bias_t[w, h // 2, :, pl.ds((h % 2) * QW, QW)] = part.T
    rows = jnp.concatenate([rows_ref[w] for w in range(GROUP)], axis=1)
    projected = dot_nt(token_t[...], tokens[...]).astype(BF16)
    which = rows[3:4, :] + lax.broadcasted_iota(jnp.int32, (1, wide), 1) // QW * TOKW
    token_ids = lax.broadcasted_iota(jnp.int32, (GROUP * TOKW, wide), 0).astype(F32)
    one_hot = jnp.where(token_ids == which, 1.0, 0.0).astype(BF16)
    condition = dot(projected, one_hot) + jnp.concatenate(
        [dot_nt(one, single_s[w]) for w in range(GROUP)], axis=1
    )
    rest, scale = centred(condition)
    gains = jnp.concatenate([gain_b[...]] * GROUP, axis=1)
    cond_s[0:QW, :] = (rest * scale * gains).astype(BF16)
    fill = lax.broadcasted_iota(jnp.int32, (QW, wide), 0)
    cond_s[QW : 2 * QW, :] = jnp.where((fill == 0) | (fill == 8) | (fill == 16), 1.0, 0.0).astype(BF16)
    high, middle, low = split(rows)
    parts = jnp.concatenate([high, high, high, middle, middle, low], axis=0).astype(BF16)
    stream_s[...] = condition + dot(position_l[...], parts)

    def block(b, carry):
        def ada_term(j):
            return dot(ada_t[b, pl.ds(j * QW, QW), :], cond_s[...])

        stream = stream_s[...]
        rest, scale = centred(stream)
        normed = ((rest * (0.5 * scale)) * (1.0 + jnp.tanh(ada_term(0))) + ada_term(1)).astype(BF16)
        query = (dot(attn_t[b, 0:QW, :], normed) * HEAD_DIM**-0.5).astype(BF16)
        key = dot(attn_t[b, QW : 2 * QW, :], normed).astype(BF16)
        value = dot(attn_t[b, 2 * QW : 3 * QW, :], normed).astype(BF16)
        gate = 1.0 + jnp.tanh(dot(attn_t[b, 3 * QW : 4 * QW, :], normed))
        ones = jnp.ones((16, QW), BF16)
        attended = []
        for w in range(GROUP):
            lanes = slice(w * QW, (w + 1) * QW)
            left = jnp.concatenate([key[:, lanes].T, one], axis=1)
            outs = []
            for pair in range(2):
                columns = []
                for h in (2 * pair, 2 * pair + 1):
                    pieces = [jnp.zeros((HEAD_DIM, QW), BF16)] * HEADS
                    pieces[h] = query[h * HEAD_DIM : (h + 1) * HEAD_DIM, lanes]
                    columns.append(jnp.concatenate(pieces, axis=0))
                right = jnp.concatenate(
                    [jnp.concatenate(columns, axis=1), bias_t[w, pair]], axis=0
                )
                scores = dot(left, right)
                exponent = jnp.exp(scores - jnp.max(scores, axis=0, keepdims=True)).astype(BF16)
                values = jnp.concatenate([value[64 * pair : 64 * pair + 64, lanes], ones], axis=0)
                product = dot(values, exponent)
                inverse = 1.0 / product[64:65, :]
                outs.append(product[0:32, 0:QW] * inverse[:, 0:QW])
                outs.append(product[32:64, QW : 2 * QW] * inverse[:, QW : 2 * QW])
            attended.append((jnp.concatenate(outs, axis=0) * gate[:, lanes]).astype(BF16))
        update = dot(out_t[b], jnp.concatenate(attended, axis=1))
        stream = stream + update * (1.0 + jnp.tanh(ada_term(2)))
        rest, scale = centred(stream)
        normed = ((rest * (0.5 * scale)) * (1.0 + jnp.tanh(ada_term(3))) + ada_term(4)).astype(BF16)
        gate_half = dot(gateup_t[b, 0 : 2 * QW, :], normed)
        up = dot(gateup_t[b, 2 * QW : 4 * QW, :], normed)
        hidden = (gate_half * up * (1.0 + jnp.tanh(gate_half))).astype(BF16)
        stream_s[...] = stream + dot(down_t[b], hidden) * (1.0 + jnp.tanh(ada_term(5)))
        return carry

    lax.fori_loop(0, BLOCKS, block, 0)
    rest, scale = centred(stream_s[...])
    update = dot(final[...], (rest * scale).astype(BF16))
    for w in range(GROUP):
        result[w] = update[0:8, w * QW : (w + 1) * QW]


def run_network(core, single_own, single_other, tokens, rows, pair_bias, bias_other, weights, final):
    half = rows.shape[0]
    steps = half // GROUP
    hidden = weights[6].shape[-1]

    def whole(array):
        return pl.BlockSpec(array.shape, lambda s, c: (0,) * array.ndim)

    own = lambda s, c: (c[0] * steps + s, 0, 0)
    there = lambda s, c: (s, 0, 0)
    return pl.pallas_call(
        network,
        grid_spec=pltpu.PrefetchScalarGridSpec(
            num_scalar_prefetch=1,
            grid=(steps,),
            in_specs=[
                pl.BlockSpec((GROUP, QW // 2, QW), own),
                pl.BlockSpec((GROUP, QW // 2, QW), there),
                pl.BlockSpec((GROUP * TOKW, tokens.shape[1]), lambda s, c: (c[0] * steps + s, 0)),
                pl.BlockSpec((GROUP, 8, QW), there),
                pl.BlockSpec((2, GROUP, QW, QW), lambda s, c: (0, c[0] * steps + s, 0, 0)),
                pl.BlockSpec((2, GROUP, QW, QW), lambda s, c: (0, s, 0, 0)),
            ]
            + [whole(array) for array in weights]
            + [whole(final)],
            out_specs=pl.BlockSpec((GROUP, 8, QW), there),
            scratch_shapes=[
                pltpu.VMEM((BLOCKS, 6 * QW, 2 * QW), BF16),
                pltpu.VMEM((BLOCKS, 4 * QW, QW), BF16),
                pltpu.VMEM((BLOCKS, QW, QW), BF16),
                pltpu.VMEM((BLOCKS, 2 * hidden, QW), BF16),
                pltpu.VMEM((BLOCKS, QW, hidden), BF16),
                pltpu.VMEM((QW, tokens.shape[1]), BF16),
                pltpu.VMEM((QW, 48), BF16),
                pltpu.VMEM((QW, QW), F32),
                pltpu.VMEM((GROUP, QW, QW), BF16),
                pltpu.VMEM((GROUP, 2, QW, 2 * QW), BF16),
                pltpu.VMEM((2 * QW, GROUP * QW), BF16),
                pltpu.VMEM((QW, GROUP * QW), F32),
            ],
        ),
        out_shape=jax.ShapeDtypeStruct((half, 8, QW), F32),
        compiler_params=pltpu.CompilerParams(vmem_limit_bytes=48 * 1024 * 1024),
    )(core, single_own, single_other, tokens, rows, pair_bias, bias_other, *weights, final)


def local(
    coords,
    noise,
    sigma,
    atom_single,
    token_single,
    atom_token,
    window_count,
    pair_bias,
    token_weight,
    cond_gain,
    position_weight,
    ada_weight,
    ada_bias,
    attn_weight,
    out_weight,
    gateup_weight,
    down_weight,
    final_weight,
    *,
    win_total,
):
    swap = [(0, 1), (1, 0)]
    core = lax.axis_index("head")
    device_id = lax.axis_index("win")
    slot_total, quarter = atom_token.shape
    half = slot_total // 2
    first_own, first_other = core * half, (1 - core) * half

    def other_half(array, axis):
        return lax.dynamic_slice_in_dim(array, first_other, half, axis)

    def own_half(array, axis):
        return lax.dynamic_slice_in_dim(array, first_own, half, axis)

    def swapped(array):
        return lax.ppermute(array, "head", swap)

    def ordered(own, other, axis):
        return jnp.where(
            core == 0,
            jnp.concatenate([own, other], axis=axis),
            jnp.concatenate([other, own], axis=axis),
        )

    sigma_value = sigma[0]
    noisy = coords + sigma_value * noise
    live_mask = (jnp.arange(slot_total, dtype=jnp.int32) < window_count[device_id]).astype(F32)
    partial = jnp.sum(noisy * live_mask[None, :, None], axis=(1, 2))
    packed = jnp.concatenate([noisy, atom_token.astype(F32)[None]], axis=0)
    packed_other = swapped(other_half(packed, 1))
    total = jnp.zeros((8, QW), F32).at[0:3, :].set(partial[:, None])
    total = total + swapped(total)
    step = 1
    while step < win_total:
        total = total + lax.ppermute(total, "win", [(i, i ^ step) for i in range(win_total)])
        step *= 2
    centre = total[0:3, 0] / (QW * jnp.sum(window_count).astype(F32))

    bias_other = swapped(other_half(pair_bias, 1))
    single_other = swapped(other_half(atom_single, 0))
    attn_other = swapped(attn_weight)
    out_other = swapped(out_weight)

    inverse = 1.0 / (1.0 + sigma_value * sigma_value)
    rows = ordered(own_half(packed, 1), packed_other, 2)
    shifted = rows[0:3] - centre[:, None, None]
    scaled = shifted * jnp.sqrt(inverse)
    rows = jnp.concatenate([scaled, rows[3:4], jnp.zeros((4, half, QW), F32)], axis=0)
    rows = jnp.transpose(rows, (1, 0, 2))
    weights = (
        ada_weight,
        ada_bias,
        attn_weight,
        attn_other,
        out_weight,
        out_other,
        gateup_weight,
        down_weight,
        token_weight,
        jnp.zeros((8, QW), F32).at[0:3].set(position_weight),
        cond_gain.reshape(QW, 1),
    )
    final = jnp.zeros((16, QW), BF16).at[0:3].set(final_weight)
    update = run_network(
        core.reshape(1).astype(jnp.int32),
        atom_single, single_other, token_single, rows, pair_bias, bias_other, weights, final,
    )
    update = jnp.transpose(update[:, 0:3], (1, 0, 2))
    denoised = shifted * inverse + sigma_value * jnp.sqrt(inverse) * update
    denoised = denoised * own_half(live_mask, 0)[None, :, None]
    mine = lax.dynamic_slice_in_dim(denoised, core * quarter, quarter, 2)
    theirs = lax.dynamic_slice_in_dim(denoised, (1 - core) * quarter, quarter, 2)
    return ordered(mine, swapped(theirs), 1)


def solution(mesh):
    placed = (
        P(None, "win", "head"),
        P(None, "win", "head"),
        P(),
        P("win", "head", None),
        P("win", None),
        P("win", "head"),
        P(),
        P("head", "win", None, None),
        P(),
        P(),
        P(),
        P(),
        P(),
        P(None, None, None, "head"),
        P(None, "head", None),
        P(),
        P(),
        P(),
    )
    return jax.shard_map(
        functools.partial(local, win_total=mesh.shape["win"]),
        mesh=mesh,
        in_specs=placed,
        out_specs=P(None, "win", "head"),
        check_vma=False,
    )
```

time: 159 us -> 75.4 us (0.47)
  blocking collectives: 55.2 us -> 0 us
  matrix products: 44.6 us -> 0 us
  Pallas kernels: 0 us -> 33.2 us
  other arithmetic: 23.5 us -> 6.42 us
  waiting for transfers between devices: 0.01 us -> 8.15 us
  local copies, waits for them, and re-layouts: 20.9 us -> 14.3 us
    dot_general x25 -> x0, matrix products: 44.6 us -> none  [the longest x3 9.03 us: window_net(): jnp.einsum('wqh,hc->wqc', hidden, down_weight[block_index], preferred_ele...]
    psum x1 -> x0, blocking collectives: 42 us -> none  [local(): totals = lax.psum(partial_pos, ('win', 'head'))]
    pallas_call x0 -> x1, Pallas kernels: none -> 33.2 us  [run_network(): pl.pallas_call(network, grid_spec=pltpu.PrefetchScalarGridSpec(num_scalar...]
    sub x3 -> x0, other arithmetic: 12 us -> none  [window_net(): exponent = jnp.exp(scores - row_max)]
    all_to_all x3 -> x0, starting transfers between devices: 11.7 us -> none  [the longest x1 4.97 us: run_net(): lax.all_to_all(pair_terms, 'head', split_axis=1, concat_axis=0, tiled=True)]
    ppermute x0 -> x11, starting transfers between devices: none -> 11.1 us  [the longest x4 9.75 us: local(): lax.ppermute(total, 'win', [(i, i ^ step) for i in range(win_total)])]
    all_to_all x2 -> x0, blocking collectives: 8.95 us -> none  [the longest x1 5.22 us: run_net(): lax.all_to_all(single, 'head', split_axis=0, concat_axis=1, tiled=True)]
    unnamed x49 -> x27, local copies, waits for them, and re-layouts: 12.6 us -> 4.16 us
  transfers between devices with their start and end apart: 3 -> 11, of which waited for: 0 -> 4; matrix products, arithmetic and copies ran while one was open for 13% -> 19% of each run, Pallas kernels for 0% -> 0%
where the time goes in v1:
time: 75.4 us; the launch traced here: 74.8 us
  Pallas kernels  33.2 us (44%)
  local copies, waits for them, and re-layouts  14.3 us (19%)
  starting transfers between devices  11.1 us (15%)
  waiting for transfers between devices  8.15 us (11%)
  other arithmetic  6.42 us (9%)
  between operations  1.56 us (2%)
    pallas_call x1, Pallas kernels, run_network(): pl.pallas_call(network, grid_spec=pltpu.PrefetchScalarGridSpec(num_scalar...  33.2 us
    ppermute x4, starting transfers between devices, local(): lax.ppermute(total, 'win', [(i, i ^ step) for i in range(win_total)])  9.75 us
    ppermute x4, waiting for transfers between devices, local(): lax.ppermute(total, 'win', [(i, i ^ step) for i in range(win_total)])  6.99 us
    unnamed x27, local copies, waits for them, and re-layouts  4.16 us
    dynamic_slice x2, local copies, waits for them, and re-layouts, other_half(): return lax.dynamic_slice_in_dim(array, first_other, half, axis)  3.19 us
    add x3, other arithmetic, local(): total + lax.ppermute(total, 'win', [(i, i ^ step) for i in range(win_tota...  1.52 us
  transfers between devices with their start and end apart: 11, of which 4 were waited for; matrix products, arithmetic and copies ran while one was open for 19% of the time, Pallas kernels for 0%

profile of v1, /device:TPU:0, one launch (start us, length us, event | category | flops | bytes accessed | tf_op | source)
XLA Modules:
  0.0 74.8 jit_solution(3088960863416519314)
XLA Ops:
  0.0 1.3 %dynamic_slice.26 = s32[1]{0:T(128)} dynamic-slice(s32[16]{0:T(128)} %param.30, s32[]{:T(128)S(6)} %select_n.39), dynamic_slice_sizes={1} | dynamic-slice | bytes 12 | tf_op jit(solution)/shard_map/dynamic_slice | solution.py:303
  2.6 1.0 %multiply_reduce_fusion = (f32[3]{0:T(128)S(1)}, f32[3,32,64]{2,0,1:T(4,128)S(1)}) fusion(f32[32]{0:T(128)S(1)} %compare_convert_fusion, f32[3,32,64]{2,1,0:T(8,128)} %param.25, f32[]{:T(128)} %bitcast.15, f32[3,32,64]{2,1,0:T(8,128)} %param.24), kind=kLoop, calls=%fused_computation.7 | loop fusion | flops 24573 | bytes 73872 | tf_op jit(solution)/shard_map/reduce_sum | solution.py:304
  4.3 2.4 %constant_dynamic-slice_fusion.2 = bf16[2,16,128,128]{3,2,1,0:T(8,128)(2,1)} fusion(bf16[2,32,128,128]{3,2,1,0:T(8,128)(2,1)} %bias_own.1, s32[]{:T(128)S(6)} %select_n.37), kind=kLoop, calls=%fused_computation.21 | loop fusion | bytes 2097156 | tf_op jit(solution)/shard_map/dynamic_slice | solution.py:286
  7.2 3.0 %collective-permute-start.2 = (f32[8,128]{0,1:T(8,128)S(1)}, f32[8,128]{0,1:T(8,128)S(1)}, u32[]{:S(2)}, u32[]{:S(2)}) collective-permute-start(f32[8,128]{0,1:T(8,128)S(1)} %add.59), channel_id=1, source_target_pairs={{0,2},{2,0},{4,6},{6,4},{8,10},{10,8},{12,14},{14,12},{16,18},{18,... | collective-permute-start | bytes 12296 | tf_op jit(solution)/shard_map/ppermute | solution.py:311
  10.2 2.3 %collective-permute-done.2 = f32[8,128]{0,1:T(8,128)S(1)} collective-permute-done((f32[8,128]{0,1:T(8,128)S(1)}, f32[8,128]{0,1:T(8,128)S(1)}, u32[]{:S(2)}, u32[]{:S(2)}) %collective-permute-start.2) | collective-permute-done | bytes 4128 | tf_op jit(solution)/shard_map/ppermute | solution.py:311
  12.5 2.1 %collective-permute-start.3 = (f32[8,128]{0,1:T(8,128)S(1)}, f32[8,128]{0,1:T(8,128)S(1)}, u32[]{:S(2)}, u32[]{:S(2)}) collective-permute-start(f32[8,128]{0,1:T(8,128)S(1)} %add.60), channel_id=1, source_target_pairs={{0,4},{2,6},{4,0},{6,2},{8,12},{10,14},{12,8},{14,10},{16,20},{18,... | collective-permute-start | bytes 12296 | tf_op jit(solution)/shard_map/ppermute | solution.py:311
  15.2 1.6 %collective-permute-done.3 = f32[8,128]{0,1:T(8,128)S(1)} collective-permute-done((f32[8,128]{0,1:T(8,128)S(1)}, f32[8,128]{0,1:T(8,128)S(1)}, u32[]{:S(2)}, u32[]{:S(2)}) %collective-permute-start.3) | collective-permute-done | bytes 4128 | tf_op jit(solution)/shard_map/ppermute | solution.py:311
  17.5 2.0 %collective-permute-start.4 = (f32[8,128]{0,1:T(8,128)}, f32[8,128]{0,1:T(8,128)}, u32[]{:S(2)}, u32[]{:S(2)}) collective-permute-start(f32[8,128]{0,1:T(8,128)} %add.61), channel_id=1, source_target_pairs={{0,8},{2,10},{4,12},{6,14},{8,0},{10,2},{12,4},{14,6},{16,24},{18,... | collective-permute-start | bytes 12296 | tf_op jit(solution)/shard_map/ppermute | solution.py:311
  19.5 0.7 constant_dynamic-slice_fusion.3
  20.3 1.1 %copy.29.attn_own = bf16[3,4,128,64]{3,2,1,0:T(8,128)(2,1)S(1)} copy(bf16[3,4,128,64]{2,3,1,0:T(8,128)(2,1)} %param.37) | data formatting | bytes 393216 | tf_op args[13]
  24.0 0.8 %copy.30.gain = f32[128,1]{1,0:T(8,128)S(1)} copy(f32[128,1]{0,1:T(1,128)} %bitcast.20) | data formatting | bytes 1024 | tf_op jit(solution)/shard_map/reshape | solution.py:337
  24.7 1.3 %scatter.19.position = f32[8,128]{1,0:T(8,128)} pad(f32[3,128]{1,0:T(4,128)} %param.34, f32[]{:T(128)} %constant.91.clone.1), padding=0_5x0_0 | pad | bytes 5636 | tf_op jit(solution)/shard_map/scatter | solution.py:336
  26.7 1.3 %scatter.20.final = bf16[16,128]{1,0:T(8,128)(2,1)} pad(bf16[3,128]{1,0:T(4,128)(2,1)} %param.41, bf16[]{:T(256)} %constant.94.clone.1), padding=0_13x0_0 | pad | bytes 4866 | tf_op jit(solution)/shard_map/scatter | solution.py:339
  28.0 0.9 %add.62 = f32[8,128]{0,1:T(8,128)S(1)} add(f32[8,128]{0,1:T(8,128)} %add.61, f32[8,128]{0,1:T(8,128)} %collective-permute-done.4) | non-fusion elementwise | flops 1024 | bytes 12288 | tf_op jit(solution)/shard_map/add | solution.py:311
  28.9 2.7 %collective-permute-start.5 = (f32[8,128]{0,1:T(8,128)S(1)}, f32[8,128]{0,1:T(8,128)S(1)}, u32[]{:S(2)}, u32[]{:S(2)}) collective-permute-start(f32[8,128]{0,1:T(8,128)S(1)} %add.62), channel_id=1, source_target_pairs={{0,16},{2,18},{4,20},{6,22},{8,24},{10,26},{12,28},{14,30},{16,0},... | collective-permute-start | bytes 12296 | tf_op jit(solution)/shard_map/ppermute | solution.py:311
  31.5 0.9 %maximum_select_fusion.1 = f32[4,16,128]{2,0,1:T(4,128)S(1)} fusion(f32[4,16,64]{2,0,1:T(4,128)} %collective-permute-done, f32[4,16,64]{2,0,1:T(4,128)} %get-tuple-element.43, pred[]{:T(512)S(6)} %eq.4), kind=kLoop, calls=%fused_computation.17 | loop fusion | flops 24576 | bytes 65537 | tf_op jit(solution)/shard_map/jit(_where)/select_n | solution.py:295
  32.5 3.1 %collective-permute-done.5 = f32[8,128]{0,1:T(8,128)S(1)} collective-permute-done((f32[8,128]{0,1:T(8,128)S(1)}, f32[8,128]{0,1:T(8,128)S(1)}, u32[]{:S(2)}, u32[]{:S(2)}) %collective-permute-start.5) | collective-permute-done | bytes 4128 | tf_op jit(solution)/shard_map/ppermute | solution.py:311
  35.6 0.7 %maximum_bitcast_fusion.rows_ref = f32[16,8,128]{2,1,0:T(8,128)S(1)} fusion(f32[1,16,128]{2,0,1:T(1,128)S(1)} %slice.68, f32[3,16,128]{2,0,1:T(4,128)S(1)} %fusion.5, f32[8]{0:T(128)} %pad.15.clone), kind=kLoop, calls=%fused_computation.3 | loop fusion | flops 32768 | bytes 98336 | tf_op jit(solution)/shard_map/transpose | solution.py:325
  36.5 0.9 %copy-done.4 = bf16[3,256,128]{2,1,0:T(8,128)(2,1)S(1)} copy-done((bf16[3,256,128]{2,1,0:T(8,128)(2,1)S(1)}, bf16[3,256,128]{2,1,0:T(8,128)(2,1)}, u32[]{:S(2)}) %copy-start.4) | copy-done | bytes 196632
  37.4 0.7 copy-done.7
  38.1 0.7 copy-done.8
  38.7 0.7 copy-done.9
  39.4 33.2 %shard_map.172 = f32[16,8,128]{2,1,0:T(8,128)S(1)} custom-call(s32[1]{0:T(128)} %bitcast.4.core_ref, bf16[32,64,128]{2,1,0:T(8,128)(2,1)S(1)} %copy-done, bf16[16,64,128]{2,1,0:T(8,128)(2,1)} %collective-permute-done.6.single_other, bf16[512,384]{1,0:T(8,128)(2,1)S(1)} %copy-done.2, f32[16,8,128]{2,1,0:T(8,128)S(1)} %maximum_bitcast_fusion.rows_ref, ...), custom_call_target="tpu_custom_call" | custom-call | tf_op jit(solution)/shard_map/pallas_call | solution.py:220
  73.0 1.1 %collective-permute-done.10 = f32[3,16,64]{2,0,1:T(4,128)S(1)} collective-permute-done((f32[3,16,64]{2,0,1:T(4,128)S(1)}, f32[3,16,64]{2,0,1:T(4,128)S(1)}, u32[]{:S(2)}, u32[]{:S(2)}) %collective-permute-start.10) | collective-permute-done | bytes 12320 | tf_op jit(solution)/shard_map/ppermute | solution.py:292
  (56 shorter events, 6.6 us)
Async XLA Ops:
  0.0 10.2 %copy-start.10 = (s32[32,64]{1,0:T(8,128)S(1)}, s32[32,64]{1,0:T(8,128)}, u32[]{:S(2)}) copy-start(s32[32,64]{1,0:T(8,128)} %param.29) | copy-start | bytes 24580
  0.0 19.5 %copy-start = (bf16[32,64,128]{2,1,0:T(8,128)(2,1)S(1)}, bf16[32,64,128]{2,1,0:T(8,128)(2,1)}, u32[]{:S(2)}) copy-start(bf16[32,64,128]{2,1,0:T(8,128)(2,1)} %single_own.1) | copy-start | bytes 1572868
  3.6 18.3 %copy-start.12 = (s32[16]{0:T(128)S(1)}, s32[16]{0:T(128)}, u32[]{:S(2)}) copy-start(s32[16]{0:T(128)} %param.30) | copy-start | bytes 196
  3.7 3.1 %collective-permute-start.1 = (f32[8,128]{0,1:T(8,128)S(1)}, f32[8,128]{0,1:T(8,128)S(1)}, u32[]{:S(2)}, u32[]{:S(2)}) collective-permute-start(f32[8,128]{0,1:T(8,128)S(1)} %broadcast.71), channel_id=1, source_target_pairs={{0,1},{1,0},{2,3},{3,2},{4,5},{5,4},{6,7},{7,6},{8,9},{9,8},{10,11... | collective-permute-start | bytes 12296 | tf_op jit(solution)/shard_map/ppermute | solution.py:292
  4.2 23.7 %copy-start.6 = (bf16[3,64,128]{2,1,0:T(8,128)(2,1)S(1)}, bf16[3,64,128]{2,1,0:T(8,128)(2,1)}, u32[]{:S(2)}) copy-start(bf16[3,64,128]{2,1,0:T(8,128)(2,1)} %out_own.1) | copy-start | bytes 147460
  4.2 32.2 %copy-start.1 = (bf16[3,6,128,128]{3,2,1,0:T(8,128)(2,1)S(1)}, bf16[3,6,128,128]{3,2,1,0:T(8,128)(2,1)}, u32[]{:S(2)}) copy-start(bf16[3,6,128,128]{3,2,1,0:T(8,128)(2,1)} %ada.1) | copy-start | bytes 1769476
  4.2 32.2 %copy-start.2 = (bf16[512,384]{1,0:T(8,128)(2,1)S(1)}, bf16[512,384]{1,0:T(8,128)(2,1)}, u32[]{:S(2)}) copy-start(bf16[512,384]{1,0:T(8,128)(2,1)} %tokens.1) | copy-start | bytes 1179652
  4.2 32.2 %copy-start.3 = (bf16[3,2,128,256]{3,2,1,0:T(8,128)(2,1)S(1)}, bf16[3,2,128,256]{3,2,1,0:T(8,128)(2,1)}, u32[]{:S(2)}) copy-start(bf16[3,2,128,256]{3,2,1,0:T(8,128)(2,1)} %gateup.1) | copy-start | bytes 1179652
  4.2 32.2 %copy-start.5 = (bf16[384,128]{1,0:T(8,128)(2,1)S(1)}, bf16[384,128]{1,0:T(8,128)(2,1)}, u32[]{:S(2)}) copy-start(bf16[384,128]{1,0:T(8,128)(2,1)} %token_.1) | copy-start | bytes 294916
  6.7 29.7 %collective-permute-start.7 = (bf16[2,16,128,128]{3,2,1,0:T(8,128)(2,1)}, bf16[2,16,128,128]{3,2,1,0:T(8,128)(2,1)S(1)}, u32[]{:S(2)}, u32[]{:S(2)}) collective-permute-start(bf16[2,16,128,128]{3,2,1,0:T(8,128)(2,1)} %constant_dynamic-slice_fusion.2), channel_id=1, source_target_pairs={{0,1},{1,0},{2,3},{3,2},{4,5},{5,4},{6,7},{7,6},{8,9},{9,8},{10,11... | collective-permute-start | bytes 3145736 | tf_op jit(solution)/shard_map/ppermute | solution.py:292
  7.2 5.3 %collective-permute-start.2 = (f32[8,128]{0,1:T(8,128)S(1)}, f32[8,128]{0,1:T(8,128)S(1)}, u32[]{:S(2)}, u32[]{:S(2)}) collective-permute-start(f32[8,128]{0,1:T(8,128)S(1)} %add.59), channel_id=1, source_target_pairs={{0,2},{2,0},{4,6},{6,4},{8,10},{10,8},{12,14},{14,12},{16,18},{18,... | collective-permute-start | bytes 12296 | tf_op jit(solution)/shard_map/ppermute | solution.py:311
  12.5 4.3 %collective-permute-start.3 = (f32[8,128]{0,1:T(8,128)S(1)}, f32[8,128]{0,1:T(8,128)S(1)}, u32[]{:S(2)}, u32[]{:S(2)}) collective-permute-start(f32[8,128]{0,1:T(8,128)S(1)} %add.60), channel_id=1, source_target_pairs={{0,4},{2,6},{4,0},{6,2},{8,12},{10,14},{12,8},{14,10},{16,20},{18,... | collective-permute-start | bytes 12296 | tf_op jit(solution)/shard_map/ppermute | solution.py:311
  15.2 13.6 %collective-permute-start = (f32[4,16,64]{2,0,1:T(4,128)}, f32[4,16,64]{2,0,1:T(4,128)}, u32[]{:S(2)}, u32[]{:S(2)}) collective-permute-start(f32[4,16,64]{2,0,1:T(4,128)} %get-tuple-element.44), channel_id=1, source_target_pairs={{0,1},{1,0},{2,3},{3,2},{4,5},{5,4},{6,7},{7,6},{8,9},{9,8},{10,11... | collective-permute-start | bytes 49160 | tf_op jit(solution)/shard_map/ppermute | solution.py:292
  17.5 10.5 %collective-permute-start.4 = (f32[8,128]{0,1:T(8,128)}, f32[8,128]{0,1:T(8,128)}, u32[]{:S(2)}, u32[]{:S(2)}) collective-permute-start(f32[8,128]{0,1:T(8,128)} %add.61), channel_id=1, source_target_pairs={{0,8},{2,10},{4,12},{6,14},{8,0},{10,2},{12,4},{14,6},{16,24},{18,... | collective-permute-start | bytes 12296 | tf_op jit(solution)/shard_map/ppermute | solution.py:311
  20.3 16.1 %collective-permute-start.6 = (bf16[16,64,128]{2,1,0:T(8,128)(2,1)}, bf16[16,64,128]{2,1,0:T(8,128)(2,1)}, u32[]{:S(2)}, u32[]{:S(2)}) collective-permute-start(bf16[16,64,128]{2,1,0:T(8,128)(2,1)} %constant_dynamic-slice_fusion.3), channel_id=1, source_target_pairs={{0,1},{1,0},{2,3},{3,2},{4,5},{5,4},{6,7},{7,6},{8,9},{9,8},{10,11... | collective-permute-start | bytes 786440 | tf_op jit(solution)/shard_map/ppermute | solution.py:292
  21.4 15.0 %collective-permute-start.8 = (bf16[3,4,128,64]{3,2,1,0:T(8,128)(2,1)S(1)}, bf16[3,4,128,64]{3,2,1,0:T(8,128)(2,1)}, u32[]{:S(2)}, u32[]{:S(2)}) collective-permute-start(bf16[3,4,128,64]{3,2,1,0:T(8,128)(2,1)S(1)} %copy.29.attn_own), channel_id=1, source_target_pairs={{0,1},{1,0},{2,3},{3,2},{4,5},{5,4},{6,7},{7,6},{8,9},{9,8},{10,11... | collective-permute-start | bytes 589832 | tf_op jit(solution)/shard_map/ppermute | solution.py:292
  27.9 8.4 %collective-permute-start.9 = (bf16[3,64,128]{2,1,0:T(8,128)(2,1)S(1)}, bf16[3,64,128]{2,1,0:T(8,128)(2,1)S(1)}, u32[]{:S(2)}, u32[]{:S(2)}) collective-permute-start(bf16[3,64,128]{2,1,0:T(8,128)(2,1)S(1)} %copy-done.6), channel_id=1, source_target_pairs={{0,1},{1,0},{2,3},{3,2},{4,5},{5,4},{6,7},{7,6},{8,9},{9,8},{10,11... | collective-permute-start | bytes 147464 | tf_op jit(solution)/shard_map/ppermute | solution.py:292
  28.9 6.7 %collective-permute-start.5 = (f32[8,128]{0,1:T(8,128)S(1)}, f32[8,128]{0,1:T(8,128)S(1)}, u32[]{:S(2)}, u32[]{:S(2)}) collective-permute-start(f32[8,128]{0,1:T(8,128)S(1)} %add.62), channel_id=1, source_target_pairs={{0,16},{2,18},{4,20},{6,22},{8,24},{10,26},{12,28},{14,30},{16,0},... | collective-permute-start | bytes 12296 | tf_op jit(solution)/shard_map/ppermute | solution.py:311
  36.4 0.9 %copy-start.4 = (bf16[3,256,128]{2,1,0:T(8,128)(2,1)S(1)}, bf16[3,256,128]{2,1,0:T(8,128)(2,1)}, u32[]{:S(2)}) copy-start(bf16[3,256,128]{2,1,0:T(8,128)(2,1)} %down.1) | copy-start | bytes 589828
  37.4 0.7 copy-start.7
  38.1 0.7 copy-start.8
  38.7 0.7 copy-start.9
  39.4 33.2 %copy-start.11 = (f32[16]{0:T(128)S(1)}, f32[16]{0:T(128)}, u32[]{:S(2)}) copy-start(f32[16]{0:T(128)} %dynamic_slice.29) | copy-start | bytes 196
  72.9 1.3 %collective-permute-start.10 = (f32[3,16,64]{2,0,1:T(4,128)S(1)}, f32[3,16,64]{2,0,1:T(4,128)S(1)}, u32[]{:S(2)}, u32[]{:S(2)}) collective-permute-start(f32[3,16,64]{2,0,1:T(4,128)S(1)} %get-tuple-element.46), channel_id=1, source_target_pairs={{0,1},{1,0},{2,3},{3,2},{4,5},{5,4},{6,7},{7,6},{8,9},{9,8},{10,11... | collective-permute-start | bytes 36872 | tf_op jit(solution)/shard_map/ppermute | solution.py:292
